TPU v7x, 128 devices: a whole 4x4x4 slice. The times are simulated.
128 devices in a mesh: lat: 32 (over y, z, core), lev: 4 (over x).
Axes of the slice: x: 4, y: 4, z: 4, core: 2. Of those that a mesh axis runs over, the one named last changes fastest.
Arguments:
- probes: bfloat16 [512, 2, 256, 512], P('lat', None, None, 'lev'), may hold values from -40 to 40
- legendre: bfloat16 [512, 2, 512, 256], P('lat'), may hold values from -0.25 to 0.25
- quad_weight: float32 [512], P('lat'), may hold values from 0.5 to 2
- trunc_counts: int32 [512], P('lat'), may hold values from 128 to 512, as said below
- background: float32 [2, 512, 16, 1024], P(None, 'lat'), may hold values from 0.5 to 1.5
- level_up: float32 [16], replicated, may hold values from 0.2 to 0.5
- level_down: float32 [16], replicated, may hold values from 0.1 to 0.3
- viscosity: float32 [16], replicated, may hold values from 0.5 to 4
Outputs:
- basis_out: bfloat16 [512, 2, 256, 512], P('lat', None, None, 'lev')
- factor: float32 [16, 16], replicated
Inputs may be any that keep to these rules, and one draw needn't show every extreme that they name: `trunc_counts`: wavenumbers kept on a northern latitude and on its mirror; some latitude keeps all 512.
All inputs are finite; a program needn't handle non-finite values.
Results may differ from a plain program's by a relative error of at most 0.017.
Values may be sent and summed in bfloat16 or wider, within the bound.
No kernel may reach another device: no remote copies, remote signals or barrier semaphores. Data moves between devices by JAX's collectives and lax.ppermute only.
A program may use at most 128 MiB of HBM per device.

v0:
```python
import math
import jax
import jax.numpy as jnp
from jax import lax
from jax.sharding import PartitionSpec as P

M = 512
K = 512
PROBES = 16


def make_waves(wave_count, lon_count):
    zonal_ids = lax.broadcasted_iota(jnp.int32, (wave_count, lon_count), 0)
    lon_ids = lax.broadcasted_iota(jnp.int32, (wave_count, lon_count), 1)
    phase = (zonal_ids * lon_ids % lon_count).astype(jnp.float32) * (2.0 * math.pi / lon_count)
    return jnp.stack([jnp.cos(phase), -jnp.sin(phase)], axis=1).astype(jnp.bfloat16)


def damping(wave_first, wave_count, half_degree, visc_cols):
    zonal_ids = wave_first + jnp.arange(wave_count, dtype=jnp.int32)
    degree = (
        zonal_ids[:, None, None]
        + 2 * jnp.arange(half_degree, dtype=jnp.int32)[None, None, :]
        + jnp.arange(2, dtype=jnp.int32)[None, :, None]
    )
    scaled_deg = (degree * (degree + 1)).astype(jnp.float32) / float((M + K) * (M + K + 1))
    damp_one = 1.0 / (1.0 + scaled_deg[..., None] * visc_cols[None, None, None, :])
    return damp_one * damp_one


def unfold(parities):
    even_part = parities[:, 0].astype(jnp.float32)
    odd_part = parities[:, 1].astype(jnp.float32)
    return jnp.stack([even_part + odd_part, even_part - odd_part], axis=1)


def couple(grid_field, outer_coef, inner_coef, level_count, probe_count, reduce_levels):
    wave_count, _, row_count, col_count = grid_field.shape
    shaped = grid_field.reshape(wave_count, 2, row_count, level_count, 2, probe_count)
    level_total = reduce_levels(jnp.sum(shaped * inner_coef[:, None, None], axis=3))
    coupled = shaped + outer_coef[:, None, None] * level_total[:, :, :, None]
    return coupled.reshape(wave_count, 2, row_count, col_count)


def grid_pass(
    grid_field,
    wave_rows,
    gain_grid,
    keep_mask,
    weights,
    outer_coef,
    inner_coef,
    probe_count,
    promote,
    reduce_levels,
    adjoint,
):
    wave_count, _, row_count, col_count = grid_field.shape
    level_count = gain_grid.shape[2]
    if adjoint:
        grid_field = grid_field * weights[None, None, :, None]
    else:
        grid_field = couple(
            grid_field, outer_coef, inner_coef, level_count, probe_count, reduce_levels
        )
        grid_field = grid_field * keep_mask[:, None, :, None]
    operand = promote(grid_field.astype(jnp.bfloat16)).reshape(
        wave_count, 2, row_count, level_count, 2, probe_count
    )
    points = jnp.einsum(
        "mhjlcs,mci->hjlsi", operand, promote(wave_rows), preferred_element_type=jnp.float32
    )
    points = promote((points * gain_grid[:, :, :, None, :]).astype(jnp.bfloat16))
    analysed = jnp.einsum(
        "hjlsi,mci->mhjlcs", points, promote(wave_rows), preferred_element_type=jnp.float32
    )
    analysed = analysed.reshape(wave_count, 2, row_count, col_count)
    if adjoint:
        analysed = analysed * keep_mask[:, None, :, None]
        analysed = couple(analysed, outer_coef, inner_coef, level_count, probe_count, reduce_levels)
    else:
        analysed = analysed * weights[None, None, :, None]
    return jnp.stack(
        [analysed[:, 0] + analysed[:, 1], analysed[:, 0] - analysed[:, 1]], axis=1
    ).astype(jnp.bfloat16)


def to_parities(legendre, spectral):
    return jnp.einsum(
        "mpjq,mpqc->mpjc", legendre, spectral, preferred_element_type=jnp.float32
    ).astype(jnp.bfloat16)


def to_spectral(legendre, folded):
    return jnp.einsum("mpjq,mpjc->mpqc", legendre, folded, preferred_element_type=jnp.float32)


def same_values(values):
    return values


def level_sum(partial_value):
    return lax.psum(partial_value.astype(jnp.bfloat16), "lev").astype(jnp.float32)


def to_rows(parities):
    arrived = lax.all_to_all(parities, "lat", split_axis=2, concat_axis=0, tiled=True)
    return arrived


def to_waves(folded):
    arrived = lax.all_to_all(folded, "lat", split_axis=0, concat_axis=2, tiled=True)
    return arrived


def shards(
    probes, legendre, quad_weight, trunc_counts, background, level_up, level_down, viscosity
):
    lat_count = lax.axis_size("lat")
    lev_count = lax.axis_size("lev")
    lat_index = lax.axis_index("lat")
    lev_index = lax.axis_index("lev")
    wave_local = probes.shape[0]
    level_local = probes.shape[3] // (2 * PROBES)
    wave_count = wave_local * lat_count
    lon_count = 2 * wave_count
    wave_rows = make_waves(wave_count, lon_count)
    weights = quad_weight
    gain_grid = lax.dynamic_slice_in_dim(background, lev_index * level_local, level_local, 2)
    up_coef = lax.dynamic_slice_in_dim(level_up, lev_index * level_local, level_local, 0)
    down_coef = lax.dynamic_slice_in_dim(level_down, lev_index * level_local, level_local, 0)
    zonal_ids = jnp.arange(wave_count, dtype=jnp.int32)
    doubling = jnp.where(zonal_ids == 0, 1.0, 2.0).astype(jnp.float32)
    keep_mask = (zonal_ids[:, None] < trunc_counts[None, :]).astype(jnp.float32) * doubling[:, None]
    weights = weights / float(lon_count)
    grid_field = unfold(to_rows(to_parities(legendre, probes)))
    folded = grid_pass(
        grid_field,
        wave_rows,
        gain_grid,
        keep_mask,
        weights,
        up_coef,
        down_coef,
        PROBES,
        same_values,
        level_sum,
        False,
    )
    tangent = to_spectral(legendre, to_waves(folded))
    visc_cols = jnp.repeat(
        lax.dynamic_slice_in_dim(viscosity, lev_index * level_local, level_local, 0), 2 * PROBES
    )
    damping_sq = damping(lat_index * wave_local, wave_local, probes.shape[2], visc_cols)
    damped = (tangent * damping_sq).astype(jnp.bfloat16)
    grid_field = unfold(to_rows(to_parities(legendre, damped)))
    folded = grid_pass(
        grid_field,
        wave_rows,
        gain_grid,
        keep_mask,
        weights,
        down_coef,
        up_coef,
        PROBES,
        same_values,
        level_sum,
        True,
    )
    images = to_spectral(legendre, to_waves(folded))
    flattened = images.reshape(-1, PROBES)
    gram_local = lax.dot_general(
        flattened, flattened, (((0,), (0,)), ((), ())), precision=lax.Precision.HIGHEST
    )
    gram_matrix = lax.psum(gram_local, ("lat", "lev"))
    lower_factor = jnp.linalg.cholesky(gram_matrix)
    inverse = lax.linalg.triangular_solve(
        lower_factor, jnp.eye(PROBES, dtype=jnp.float32), left_side=True, lower=True
    )
    row_scale = math.sqrt(flattened.shape[0] * lat_count * lev_count)
    basis_out = (row_scale * jnp.dot(flattened, inverse.T, precision=lax.Precision.HIGHEST)).astype(
        jnp.bfloat16
    )
    basis_out = basis_out.reshape(images.shape)
    factor = lower_factor.T / row_scale
    return (basis_out, factor)


def solution(mesh):
    placed = (
        P("lat", None, None, "lev"),
        P("lat", None, None, None),
        P("lat"),
        P("lat"),
        P(None, "lat", None, None),
        P(),
        P(),
        P(),
    )
    return jax.shard_map(
        shards,
        mesh=mesh,
        in_specs=placed,
        out_specs=(P("lat", None, None, "lev"), P()),
        check_vma=False,
    )
```

profile of v0, /device:TPU:1, one launch (start us, length us, event | category | flops | bytes accessed | tf_op | source)
XLA Modules:
  0.0 726.1 jit_solution(6764757870753245017)
XLA Ops:
  8.8 5.7 convolution_convert_fusion
  14.5 6.3 copy.88
  20.8 9.8 %all-to-all-start = ((bf16[16,2,512,128]{3,1,0,2:T(2,128)(2,1)}), bf16[16,2,512,128]{3,1,0,2:T(2,128)(2,1)}, u32[]{:S(2)}, u32[]{:S(2)}) async-start(bf16[16,2,512,128]{3,1,0,2:T(2,128)(2,1)} %copy.88), calls=%async_computation | async-start | bytes 8388608 | tf_op jit(solution)/shard_map/all_to_all | solution.py:107
  31.0 51.7 %all-to-all-done = bf16[16,2,512,128]{3,1,0,2:T(2,128)(2,1)} async-done(((bf16[16,2,512,128]{3,1,0,2:T(2,128)(2,1)}), bf16[16,2,512,128]{3,1,0,2:T(2,128)(2,1)}, u32[]{:S(2)}, u32[]{:S(2)}) %all-to-all-start) | async-done | bytes 4194336 | tf_op jit(solution)/shard_map/all_to_all | solution.py:107
  102.1 5.5 multiply_reduce_fusion
  109.9 9.7 %negate_convert_fusion = (bf16[512,1,1024]{2,0,1:T(8,128)(2,1)S(1)}, bf16[512,1,1024]{2,0,1:T(8,128)(2,1)}) fusion(), kind=kLoop, calls=%fused_computation.52 | loop fusion | flops 8912896 | bytes 2097152 | tf_op jit(solution)/shard_map/convert.5
  119.6 33.0 %all-reduce.3.cloned.1.call-done = bf16[512,2,16,2,16]{0,4,2,1,3:T(8,128)(2,1)} async-done(((bf16[512,2,16,2,16]{0,4,2,1,3:T(8,128)(2,1)}), bf16[512,2,16,2,16]{0,4,2,1,3:T(8,128)(2,1)}) %all-reduce.3.cloned.1.call-update) | async-done | bytes 1048592 | tf_op jit(solution)/shard_map/psum | solution.py:103
  154.1 8.5 %fusion.14 = f32[2,16,4,16,1024,1]{4,3,0,2,1,5:T(8,128)S(1)} fusion(bf16[512,1,1024]{2,0,1:T(8,128)(2,1)S(1)} %get-tuple-element.24, bf16[512,1,1024]{2,0,1:T(8,128)(2,1)} %get-tuple-element.25, f32[512,16]{0,1:T(8,128)S(1)} %fusion.34, f32[512,2,16,2,16]{0,4,2,1,3:T(8,128)S(1)} %convert_element_type.94, f32[4]{0:T(128)S(1)} %dynamic_slice.12, ...), kind=kOutput, calls=%fused_computation.28 | convolution fusion | flops 4306501632 | bytes 21004304 | tf_op jit(solution)/shard_map/mhjlcs,mci->hjlsi/dot_general | solution.py:70
  175.3 7.9 %copy.96 = bf16[512,2,16,128]{3,2,1,0:T(8,128)(2,1)} copy(bf16[512,2,16,128]{0,3,2,1:T(8,128)(2,1)} %pad_maximum_fusion.1) | data formatting | bytes 8388608 | tf_op jit(solution)/shard_map/stack | solution.py:83
  183.3 9.7 %all-to-all-start.1 = ((bf16[512,2,16,128]{3,2,1,0:T(8,128)(2,1)}), bf16[512,2,16,128]{3,2,1,0:T(8,128)(2,1)}, u32[]{:S(2)}, u32[]{:S(2)}) async-start(bf16[512,2,16,128]{3,2,1,0:T(8,128)(2,1)} %copy.96), calls=%async_computation.1 | async-start | bytes 8388608 | tf_op jit(solution)/shard_map/all_to_all | solution.py:112
  193.4 51.7 %all-to-all-done.1 = bf16[512,2,16,128]{3,2,1,0:T(8,128)(2,1)} async-done(((bf16[512,2,16,128]{3,2,1,0:T(8,128)(2,1)}), bf16[512,2,16,128]{3,2,1,0:T(8,128)(2,1)}, u32[]{:S(2)}, u32[]{:S(2)}) %all-to-all-start.1) | async-done | bytes 4194336 | tf_op jit(solution)/shard_map/all_to_all | solution.py:112
  250.4 13.1 %convert_bitcast_fusion = bf16[16,2,512,128]{2,3,1,0:T(8,128)(2,1)} fusion(bf16[16,2,512,256]{3,2,1,0:T(8,128)(2,1)} %param.9, bf16[16,2,512,128]{3,2,1,0:T(8,128)(2,1)} %bitcast.131, f32[128]{0:T(128)S(1)} %mul.211, f32[16,2,256]{2,1,0:T(2,128)S(1)} %fusion.33), kind=kOutput, calls=%fused_computation.33 | convolution fusion | flops 2155872256 | bytes 16810496 | tf_op jit(solution)/shard_map/mpjq,mpqc->mpjc/dot_general | solution.py:89
  263.5 11.2 %copy.99 = bf16[16,2,512,128]{3,1,0,2:T(2,128)(2,1)} copy(bf16[16,2,512,128]{2,3,1,0:T(8,128)(2,1)} %convert_bitcast_fusion) | data formatting | bytes 8388608 | tf_op jit(solution)/shard_map/convert_element_type | solution.py:91
  274.7 57.9 %all_to_all.72 = bf16[16,2,512,128]{3,1,0,2:T(2,128)(2,1)S(1)} all-to-all(bf16[16,2,512,128]{3,1,0,2:T(2,128)(2,1)} %copy.99), channel_id=1, replica_groups=mesh['lat'=32,'lev'=4] {'lat'}, dimensions={2} | all-to-all | bytes 8388608 | tf_op jit(solution)/shard_map/all_to_all | solution.py:107
  349.8 14.8 %fusion.2 = (bf16[512,2,16,2,16]{0,4,2,1,3:T(8,128)(2,1)}, f32[512,2,2,16,4,16]{0,5,4,3,2,1:T(8,128)}) fusion(f32[512,16]{0,1:T(8,128)S(1)} %fusion.34, f32[4]{0:T(128)S(1)} %dynamic_slice.12, f32[2,16,4,1024]{3,2,1,0:T(4,128)S(1)} %copy-done.5, bf16[512,1,1024]{2,0,1:T(8,128)(2,1)S(1)} %get-tuple-element.24, bf16[512,1,1024]{2,0,1:T(8,128)(2,1)S(1)} %copy-done.3, ...), kind=kOutput, calls=%fused_computation.7 | convolution fusion | flops 8611430400 | bytes 20480080 | tf_op jit(solution)/shard_map/hjlsi,mci->mhjlcs/dot_general | solution.py:74
  364.6 41.5 %all-reduce.5.cloned.1.call-done = bf16[512,2,16,2,16]{0,4,2,1,3:T(8,128)(2,1)} async-done(((bf16[512,2,16,2,16]{0,4,2,1,3:T(8,128)(2,1)}), bf16[512,2,16,2,16]{0,4,2,1,3:T(8,128)(2,1)}) %all-reduce.5.cloned.1.call-update) | async-done | bytes 1048592 | tf_op jit(solution)/shard_map/psum | solution.py:103
  424.2 7.9 %copy.105 = bf16[512,2,16,128]{3,2,1,0:T(8,128)(2,1)} copy(bf16[512,2,16,128]{0,3,2,1:T(8,128)(2,1)} %pad_maximum_fusion.2) | data formatting | bytes 8388608 | tf_op jit(solution)/shard_map/stack | solution.py:83
  432.1 60.4 %all_to_all.73 = bf16[512,2,16,128]{3,2,1,0:T(8,128)(2,1)S(1)} all-to-all(bf16[512,2,16,128]{3,2,1,0:T(8,128)(2,1)} %copy.105), channel_id=1, replica_groups=mesh['lat'=32,'lev'=4] {'lat'}, dimensions={0} | all-to-all | bytes 8388608 | tf_op jit(solution)/shard_map/all_to_all | solution.py:112
  503.6 19.6 %reshape.201 = f32[65536,16]{1,0:T(8,128)} reshape(f32[16,2,256,128]{3,2,1,0:T(8,128)} %copy.108) | data formatting | bytes 8388608 | tf_op jit(solution)/shard_map/reshape | solution.py:171
  523.2 64.4 %fusion.53 = f32[16,16]{0,1:T(8,128)S(1)} fusion(f32[65536,16]{1,0:T(8,128)} %reshape.201), kind=kOutput, calls=%fused_computation.82 | convolution fusion | flops 201326592 | bytes 4195328 | tf_op jit(solution)/shard_map/dot_general | solution.py:172
  587.5 63.6 %psum.23 = f32[16,16]{0,1:T(8,128)S(1)} all-reduce(f32[16,16]{0,1:T(8,128)S(1)} %fusion.53), channel_id=1, replica_groups=mesh['lat'=32,'lev'=4] {'lat','lev'}, use_global_device_ids=true, to_apply=%region_4.5 | all-reduce | flops 256 | bytes 2048 | tf_op jit(solution)/shard_map/psum | solution.py:175
  656.1 32.9 %fusion = bf16[65536,16]{0,1:T(8,128)(2,1)S(1)} fusion(f32[65536,16]{1,0:T(8,128)} %reshape.201, f32[16,16]{1,0:T(8,128)S(1)} %fusion.35), kind=kOutput, calls=%fused_computation.1 | convolution fusion | flops 203423744 | bytes 6292480 | tf_op jit(solution)/shard_map/dot_general | solution.py:181
  689.0 11.1 %copy.111 = bf16[65536,16]{1,0:T(8,128)(2,1)} copy(bf16[65536,16]{0,1:T(8,128)(2,1)S(1)} %fusion) | data formatting | bytes 4194304 | tf_op jit(solution)/shard_map/convert_element_type | solution.py:181
  700.1 18.9 %reshape.202 = bf16[16,2,256,128]{3,2,1,0:T(8,128)(2,1)} reshape(bf16[65536,16]{1,0:T(8,128)(2,1)} %copy.111) | data formatting | bytes 4194304 | tf_op jit(solution)/shard_map/reshape | solution.py:184
  (78 shorter events, 95.0 us)
Async XLA Ops:
  7.2 1.6 copy-start
  20.8 10.1 %copy-start.7 = (f32[16]{0:T(128)S(1)}, f32[16]{0:T(128)}, u32[]{:S(2)}) copy-start(f32[16]{0:T(128)} %param.14) | copy-start | bytes 196
  20.8 61.9 %all-to-all-start = ((bf16[16,2,512,128]{3,1,0,2:T(2,128)(2,1)}), bf16[16,2,512,128]{3,1,0,2:T(2,128)(2,1)}, u32[]{:S(2)}, u32[]{:S(2)}) async-start(bf16[16,2,512,128]{3,1,0,2:T(2,128)(2,1)} %copy.88), calls=%async_computation | async-start | bytes 8388608 | tf_op jit(solution)/shard_map/all_to_all | solution.py:107
  30.6 122.0 %all-reduce.3.cloned.1.call-start = ((), (), s32[]{:S(2)}) async-start(), calls=%async_computation.4 | async-start | bytes 2097152 | tf_op jit(solution)/shard_map/psum | solution.py:103
  102.1 5.5 copy-start.8
  102.1 7.7 %copy-start.9 = (f32[16]{0:T(128)S(1)}, f32[16]{0:T(128)}, u32[]{:S(2)}) copy-start(f32[16]{0:T(128)} %param.10) | copy-start | bytes 196
  102.1 7.8 %copy-start.6 = (s32[16]{0:T(128)S(1)}, s32[16]{0:T(128)}, u32[]{:S(2)}) copy-start(s32[16]{0:T(128)} %param.11) | copy-start | bytes 196
  154.1 8.5 %copy-start.2 = (bf16[512,1,1024]{2,0,1:T(8,128)(2,1)S(1)}, bf16[512,1,1024]{2,0,1:T(8,128)(2,1)}, u32[]{:S(2)}) copy-start(bf16[512,1,1024]{2,0,1:T(8,128)(2,1)} %get-tuple-element.25) | copy-start | bytes 3145732
  154.1 8.5 %copy-start.4 = (f32[2,16,4,1024]{3,2,1,0:T(4,128)S(1)}, f32[2,16,4,1024]{3,2,1,0:T(4,128)}, u32[]{:S(2)}) copy-start(f32[2,16,4,1024]{3,2,1,0:T(4,128)} %constant_dynamic-slice_fusion) | copy-start | bytes 1572868
  183.3 9.7 %copy-start.10 = (f32[16]{0:T(128)S(1)}, f32[16]{0:T(128)}, u32[]{:S(2)}) copy-start(f32[16]{0:T(128)} %param.15) | copy-start | bytes 196
  183.3 61.8 %all-to-all-start.1 = ((bf16[512,2,16,128]{3,2,1,0:T(8,128)(2,1)}), bf16[512,2,16,128]{3,2,1,0:T(8,128)(2,1)}, u32[]{:S(2)}, u32[]{:S(2)}) async-start(bf16[512,2,16,128]{3,2,1,0:T(8,128)(2,1)} %copy.96), calls=%async_computation.1 | async-start | bytes 8388608 | tf_op jit(solution)/shard_map/all_to_all | solution.py:112
  192.9 213.2 %all-reduce.5.cloned.1.call-start = ((), (), s32[]{:S(2)}) async-start(), calls=%async_computation.5 | async-start | bytes 2097152 | tf_op jit(solution)/shard_map/psum | solution.py:103
  344.4 5.4 copy-start.3
  344.4 5.4 copy-start.5
  432.1 61.6 %slice-start = ((s8[8388608]{0:T(1024)(128)(4,1)}), s8[4194304]{0:T(1024)(128)(4,1)S(1)}, s32[]{:S(2)}) async-start(s8[8388608]{0:T(1024)(128)(4,1)} %bitcast.116), calls=%async_computation.6 | async-start | bytes 8388608
  492.5 2.2 slice-start.1
  700.1 18.9 %copy-start.1 = (bf16[16,2,256,128]{3,2,1,0:T(8,128)(2,1)S(1)}, bf16[16,2,256,128]{3,2,1,0:T(8,128)(2,1)}, u32[]{:S(2)}) copy-start(bf16[16,2,256,128]{3,2,1,0:T(8,128)(2,1)} %param.8) | copy-start | bytes 6291460
Sparse Core Ops, SparseCore 0:
  107.7 44.8 all-reduce.2
  364.8 41.2 all-reduce.4
where the time goes:
time: 734 us; the launch traced here: 726 us
  blocking collectives  182 us (25%)
  waiting for transfers between devices  178 us (24%)
  matrix products  148 us (20%)
  local copies, waits for them, and re-layouts  136 us (19%)
  other arithmetic  48.5 us (7%)
  starting transfers between devices  19.8 us (3%)
  between operations  14.5 us (2%)
    psum x2, waiting for transfers between devices, level_sum(): lax.psum(partial_value.astype(jnp.bfloat16), 'lev').astype(jnp.float32)  74.4 us
    dot_general x1, matrix products, shards(): lax.dot_general(flattened, flattened, (((0,), (0,)), ((), ())), precision...  64.4 us
    psum x1, blocking collectives, shards(): gram_matrix = lax.psum(gram_local, ('lat', 'lev'))  63.6 us
    all_to_all x1, blocking collectives, to_waves(): lax.all_to_all(folded, 'lat', split_axis=0, concat_axis=2, tiled=True)  60.4 us
    all_to_all x1, blocking collectives, to_rows(): lax.all_to_all(parities, 'lat', split_axis=2, concat_axis=0, tiled=True)  57.9 us
    all_to_all x1, waiting for transfers between devices, to_waves(): lax.all_to_all(folded, 'lat', split_axis=0, concat_axis=2, tiled=True)  51.7 us
    all_to_all x1, waiting for transfers between devices, to_rows(): lax.all_to_all(parities, 'lat', split_axis=2, concat_axis=0, tiled=True)  51.7 us
    dot_general x1, matrix products, shards(): jnp.dot(flattened, inverse.T, precision=lax.Precision.HIGHEST)  32.9 us
  transfers between devices with their start and end apart: 4, of which 4 were waited for; matrix products, arithmetic and copies ran while one was open for 2% of the time, Pallas kernels for 0%

commit v1 on v0

--- a/solution.py
+++ b/solution.py
@@ -100,7 +100,9 @@
 
 
 def level_sum(partial_value):
-    return lax.psum(partial_value.astype(jnp.bfloat16), "lev").astype(jnp.float32)
+    return jnp.sum(
+        jax.lax.all_gather(partial_value.astype(jnp.bfloat16), axis_name="lev"), axis=0
+    ).astype(jnp.float32)
 
 
 def to_rows(parities):

time: 734 us -> 768 us (1.046)
  local copies, waits for them, and re-layouts: 136 us -> 155 us
  other arithmetic: 48.5 us -> 58.2 us
  waiting for transfers between devices: 178 us -> 186 us
    all_gather x0 -> x2, waiting for transfers between devices: none -> 82.2 us  [level_sum(): jax.lax.all_gather(partial_value.astype(jnp.bfloat16), axis_name='lev')]
    psum x2 -> x0, waiting for transfers between devices: 74.4 us -> none  [level_sum(): lax.psum(partial_value.astype(jnp.bfloat16), 'lev').astype(jnp.float32)]
    all_gather x0 -> x2, local copies, waits for them, and re-layouts: none -> 16.2 us  [level_sum(): jax.lax.all_gather(partial_value.astype(jnp.bfloat16), axis_name='lev')]
    reduce_sum x0 -> x2, other arithmetic: none -> 15.1 us  [level_sum(): jnp.sum(jax.lax.all_gather(partial_value.astype(jnp.bfloat16), axis_name=...]
    dot_general x1 -> x2, matrix products: 8.5 us -> 16.4 us  [grid_pass(): jnp.einsum('mhjlcs,mci->hjlsi', operand, promote(wave_rows), preferred_el...]
where the time goes in v1:
time: 768 us; the launch traced here: 759 us
  waiting for transfers between devices  186 us (24%)
  blocking collectives  180 us (23%)
  local copies, waits for them, and re-layouts  155 us (20%)
  matrix products  148 us (19%)
  other arithmetic  58.2 us (8%)
  starting transfers between devices  18.2 us (2%)
  between operations  14.8 us (2%)
    all_gather x2, waiting for transfers between devices, level_sum(): jax.lax.all_gather(partial_value.astype(jnp.bfloat16), axis_name='lev')  82.2 us
    dot_general x1, matrix products, shards(): lax.dot_general(flattened, flattened, (((0,), (0,)), ((), ())), precision...  64.1 us
    psum x1, blocking collectives, shards(): gram_matrix = lax.psum(gram_local, ('lat', 'lev'))  63.1 us
    all_to_all x1, blocking collectives, to_waves(): lax.all_to_all(folded, 'lat', split_axis=0, concat_axis=2, tiled=True)  58.7 us
    all_to_all x1, blocking collectives, to_rows(): lax.all_to_all(parities, 'lat', split_axis=2, concat_axis=0, tiled=True)  58.1 us
    all_to_all x1, waiting for transfers between devices, to_rows(): lax.all_to_all(parities, 'lat', split_axis=2, concat_axis=0, tiled=True)  51.8 us
    all_to_all x1, waiting for transfers between devices, to_waves(): lax.all_to_all(folded, 'lat', split_axis=0, concat_axis=2, tiled=True)  51.7 us
    dot_general x1, matrix products, shards(): jnp.dot(flattened, inverse.T, precision=lax.Precision.HIGHEST)  32.9 us
  transfers between devices with their start and end apart: 4, of which 4 were waited for; matrix products, arithmetic and copies ran while one was open for 2% of the time, Pallas kernels for 0%

profile of v1, /device:TPU:1, one launch (start us, length us, event | category | flops | bytes accessed | tf_op | source)
XLA Modules:
  0.0 759.4 jit_solution(6403282785535458303)
XLA Ops:
  20.8 9.8 %all-to-all-start = ((bf16[16,2,512,128]{3,1,0,2:T(2,128)(2,1)}), bf16[16,2,512,128]{3,1,0,2:T(2,128)(2,1)}, u32[]{:S(2)}, u32[]{:S(2)}) async-start(bf16[16,2,512,128]{3,1,0,2:T(2,128)(2,1)} %copy.117), calls=%async_computation | async-start | bytes 8388608 | tf_op jit(solution)/shard_map/all_to_all | solution.py:109
  30.9 51.8 %all-to-all-done = bf16[16,2,512,128]{3,1,0,2:T(2,128)(2,1)} async-done(((bf16[16,2,512,128]{3,1,0,2:T(2,128)(2,1)}), bf16[16,2,512,128]{3,1,0,2:T(2,128)(2,1)}, u32[]{:S(2)}, u32[]{:S(2)}) %all-to-all-start) | async-done | bytes 4194336 | tf_op jit(solution)/shard_map/all_to_all | solution.py:109
  110.6 8.5 %negate_convert_fusion = (bf16[512,1,1024]{2,0,1:T(8,128)(2,1)S(1)}, bf16[512,1,1024]{2,0,1:T(8,128)(2,1)S(1)}) fusion(), kind=kLoop, calls=%fused_computation.52 | loop fusion | flops 8912896 | bytes 2097152 | tf_op jit(solution)/shard_map/convert.7
  119.1 37.5 %all-gather.5.cloned.1.call-done = bf16[2048,2,16,2,16]{0,4,3,2,1:T(8,128)(2,1)} async-done(((bf16[512,2,16,2,16]{0,4,3,2,1:T(8,128)(2,1)}), bf16[2048,2,16,2,16]{0,4,3,2,1:T(8,128)(2,1)}) %all-gather.5.cloned.1.call-update) | async-done | bytes 4194320 | tf_op jit(solution)/shard_map/all_gather | solution.py:104
  156.5 8.2 %reshape.223 = bf16[4,512,2,16,2,16]{1,0,5,4,3,2:T(4,128)(2,1)} reshape(bf16[2048,2,16,2,16]{0,4,3,2,1:T(8,128)(2,1)} %all-gather.5.cloned.1.call-done) | data formatting | bytes 8388608 | tf_op jit(solution)/shard_map/all_gather | solution.py:104
  164.8 7.6 reduce_sum.43
  172.3 8.3 %fusion.10 = f32[2,16,4,16,1024,1]{4,3,1,0,2,5:T(8,128)S(1)} fusion(bf16[512,1,1024]{2,0,1:T(8,128)(2,1)S(1)} %get-tuple-element.26, bf16[512,1,1024]{2,0,1:T(8,128)(2,1)S(1)} %get-tuple-element.27, f32[512,16]{0,1:T(8,128)S(1)} %fusion.33, f32[4]{0:T(128)S(1)} %dynamic_slice.12, bf16[512,2,16,2,16]{0,4,3,2,1:T(8,128)(2,1)S(1)} %reduce_sum.43, ...), kind=kOutput, calls=%fused_computation.27 | convolution fusion | flops 4306501632 | bytes 19955728 | tf_op jit(solution)/shard_map/mhjlcs,mci->hjlsi/dot_general | solution.py:70
  193.4 7.9 %copy.130 = bf16[512,2,16,128]{3,2,1,0:T(8,128)(2,1)} copy(bf16[512,2,16,128]{0,3,2,1:T(8,128)(2,1)} %pad_maximum_fusion.1) | data formatting | bytes 8388608 | tf_op jit(solution)/shard_map/stack | solution.py:83
  201.4 8.1 %all-to-all-start.1 = ((bf16[512,2,16,128]{3,2,1,0:T(8,128)(2,1)}), bf16[512,2,16,128]{3,2,1,0:T(8,128)(2,1)}, u32[]{:S(2)}, u32[]{:S(2)}) async-start(bf16[512,2,16,128]{3,2,1,0:T(8,128)(2,1)} %copy.130), calls=%async_computation.1 | async-start | bytes 8388608 | tf_op jit(solution)/shard_map/all_to_all | solution.py:114
  209.9 51.7 %all-to-all-done.1 = bf16[512,2,16,128]{3,2,1,0:T(8,128)(2,1)} async-done(((bf16[512,2,16,128]{3,2,1,0:T(8,128)(2,1)}), bf16[512,2,16,128]{3,2,1,0:T(8,128)(2,1)}, u32[]{:S(2)}, u32[]{:S(2)}) %all-to-all-start.1) | async-done | bytes 4194336 | tf_op jit(solution)/shard_map/all_to_all | solution.py:114
  266.9 13.1 %convert_bitcast_fusion = bf16[16,2,512,128]{2,3,1,0:T(8,128)(2,1)} fusion(bf16[16,2,512,256]{3,2,1,0:T(8,128)(2,1)} %param.9, bf16[16,2,512,128]{3,2,1,0:T(8,128)(2,1)} %bitcast.124, f32[128]{0:T(128)S(1)} %mul.211, f32[16,2,256]{2,1,0:T(2,128)S(1)} %fusion.32), kind=kOutput, calls=%fused_computation.35 | convolution fusion | flops 2155872256 | bytes 16810496 | tf_op jit(solution)/shard_map/mpjq,mpqc->mpjc/dot_general | solution.py:89
  280.1 11.2 %copy.133 = bf16[16,2,512,128]{3,1,0,2:T(2,128)(2,1)} copy(bf16[16,2,512,128]{2,3,1,0:T(8,128)(2,1)} %convert_bitcast_fusion) | data formatting | bytes 8388608 | tf_op jit(solution)/shard_map/convert_element_type | solution.py:91
  291.3 58.1 %all_to_all.72 = bf16[16,2,512,128]{3,1,0,2:T(2,128)(2,1)S(1)} all-to-all(bf16[16,2,512,128]{3,1,0,2:T(2,128)(2,1)} %copy.133), channel_id=1, replica_groups=mesh['lat'=32,'lev'=4] {'lat'}, dimensions={2} | all-to-all | bytes 8388608 | tf_op jit(solution)/shard_map/all_to_all | solution.py:109
  366.7 8.1 %fusion.3 = bf16[2,16,4,16,1024]{4,3,0,2,1:T(8,128)(2,1)S(1)} fusion(f32[2,16,4,1024]{3,0,2,1:T(2,128)S(1)} %copy-done.5, bf16[512,1,1024]{2,0,1:T(8,128)(2,1)S(1)} %get-tuple-element.26, bf16[512,1,1024]{2,0,1:T(8,128)(2,1)S(1)} %copy-done.3, f32[512,1,16,4,2,16]{0,5,4,3,2,1:T(8,128)} %bitcast.123, f32[512,1,16,4,2,16]{0,5,4,3,2,1:T(8,128)} %bitcast.122, ...), kind=kOutput, calls=%fused_computation.9 | convolution fusion | flops 4306501632 | bytes 15204416 | tf_op jit(solution)/shard_map/mhjlcs,mci->hjlsi/dot_general | solution.py:70
  382.9 44.7 %all-gather.7.cloned.1.call-done = bf16[2048,2,16,2,16]{0,4,3,2,1:T(8,128)(2,1)} async-done(((bf16[512,2,16,2,16]{0,4,3,2,1:T(8,128)(2,1)}), bf16[2048,2,16,2,16]{0,4,3,2,1:T(8,128)(2,1)}) %all-gather.7.cloned.1.call-update) | async-done | bytes 4194320 | tf_op jit(solution)/shard_map/all_gather | solution.py:104
  427.6 8.0 %reshape.224 = bf16[4,512,2,16,2,16]{1,0,5,4,3,2:T(4,128)(2,1)} reshape(bf16[2048,2,16,2,16]{0,4,3,2,1:T(8,128)(2,1)} %all-gather.7.cloned.1.call-done) | data formatting | bytes 8388608 | tf_op jit(solution)/shard_map/all_gather | solution.py:104
  459.7 7.9 %copy.143 = bf16[512,2,16,128]{3,2,1,0:T(8,128)(2,1)} copy(bf16[512,2,16,128]{0,3,2,1:T(8,128)(2,1)} %pad_maximum_fusion.2) | data formatting | bytes 8388608 | tf_op jit(solution)/shard_map/stack | solution.py:83
  467.6 58.7 %all_to_all.73 = bf16[512,2,16,128]{3,2,1,0:T(8,128)(2,1)S(1)} all-to-all(bf16[512,2,16,128]{3,2,1,0:T(8,128)(2,1)} %copy.143), channel_id=1, replica_groups=mesh['lat'=32,'lev'=4] {'lat'}, dimensions={0} | all-to-all | bytes 8388608 | tf_op jit(solution)/shard_map/all_to_all | solution.py:114
  537.4 19.6 %reshape.221 = f32[65536,16]{1,0:T(8,128)} reshape(f32[16,2,256,128]{3,2,1,0:T(8,128)} %copy.146) | data formatting | bytes 8388608 | tf_op jit(solution)/shard_map/reshape | solution.py:173
  557.0 64.1 %fusion.39 = f32[16,16]{0,1:T(8,128)S(1)} fusion(f32[65536,16]{1,0:T(8,128)} %reshape.221), kind=kOutput, calls=%fused_computation.81 | convolution fusion | flops 201326592 | bytes 4195328 | tf_op jit(solution)/shard_map/dot_general | solution.py:174
  621.1 63.1 %psum.7 = f32[16,16]{0,1:T(8,128)S(1)} all-reduce(f32[16,16]{0,1:T(8,128)S(1)} %fusion.39), channel_id=1, replica_groups=mesh['lat'=32,'lev'=4] {'lat','lev'}, use_global_device_ids=true, to_apply=%region_4.5 | all-reduce | flops 256 | bytes 2048 | tf_op jit(solution)/shard_map/psum | solution.py:177
  689.2 32.9 %fusion = bf16[65536,16]{0,1:T(8,128)(2,1)S(1)} fusion(f32[65536,16]{1,0:T(8,128)} %reshape.221, f32[16,16]{1,0:T(8,128)S(1)} %fusion.34), kind=kOutput, calls=%fused_computation.1 | convolution fusion | flops 203423744 | bytes 6292480 | tf_op jit(solution)/shard_map/dot_general | solution.py:183
  722.1 11.1 %copy.149 = bf16[65536,16]{1,0:T(8,128)(2,1)} copy(bf16[65536,16]{0,1:T(8,128)(2,1)S(1)} %fusion) | data formatting | bytes 4194304 | tf_op jit(solution)/shard_map/convert_element_type | solution.py:183
  733.2 18.9 %reshape.222 = bf16[16,2,256,128]{3,2,1,0:T(8,128)(2,1)} reshape(bf16[65536,16]{1,0:T(8,128)(2,1)} %copy.149) | data formatting | bytes 4194304 | tf_op jit(solution)/shard_map/reshape | solution.py:186
  (84 shorter events, 125.6 us)
Async XLA Ops:
  7.2 1.6 copy-start
  20.8 10.1 %copy-start.7 = (f32[16]{0:T(128)S(1)}, f32[16]{0:T(128)}, u32[]{:S(2)}) copy-start(f32[16]{0:T(128)} %param.14) | copy-start | bytes 196
  20.8 61.9 %all-to-all-start = ((bf16[16,2,512,128]{3,1,0,2:T(2,128)(2,1)}), bf16[16,2,512,128]{3,1,0,2:T(2,128)(2,1)}, u32[]{:S(2)}, u32[]{:S(2)}) async-start(bf16[16,2,512,128]{3,1,0,2:T(2,128)(2,1)} %copy.117), calls=%async_computation | async-start | bytes 8388608 | tf_op jit(solution)/shard_map/all_to_all | solution.py:109
  30.6 126.0 %all-gather.5.cloned.1.call-start = ((), (), s32[]{:S(2)}) async-start(), calls=%async_computation.4 | async-start | bytes 5242880 | tf_op jit(solution)/shard_map/all_gather | solution.py:104
  102.1 5.7 copy-start.8
  106.6 3.8 copy-start.9
  106.6 3.8 copy-start.6
  119.1 61.6 %copy-start.2 = (bf16[512,1,1024]{2,0,1:T(8,128)(2,1)}, bf16[512,1,1024]{2,0,1:T(8,128)(2,1)S(1)}, u32[]{:S(2)}) copy-start(bf16[512,1,1024]{2,0,1:T(8,128)(2,1)S(1)} %get-tuple-element.27) | copy-start | bytes 3145732
  172.3 8.4 %copy-start.4 = (f32[2,16,4,1024]{3,0,2,1:T(2,128)S(1)}, f32[2,16,4,1024]{3,0,2,1:T(2,128)}, u32[]{:S(2)}) copy-start(f32[2,16,4,1024]{3,0,2,1:T(2,128)} %copy.127) | copy-start | bytes 1572868
  201.4 8.2 %copy-start.10 = (f32[16]{0:T(128)S(1)}, f32[16]{0:T(128)}, u32[]{:S(2)}) copy-start(f32[16]{0:T(128)} %param.15) | copy-start | bytes 196
  201.4 60.2 %all-to-all-start.1 = ((bf16[512,2,16,128]{3,2,1,0:T(8,128)(2,1)}), bf16[512,2,16,128]{3,2,1,0:T(8,128)(2,1)}, u32[]{:S(2)}, u32[]{:S(2)}) async-start(bf16[512,2,16,128]{3,2,1,0:T(8,128)(2,1)} %copy.130), calls=%async_computation.1 | async-start | bytes 8388608 | tf_op jit(solution)/shard_map/all_to_all | solution.py:114
  209.5 218.2 %all-gather.7.cloned.1.call-start = ((), (), s32[]{:S(2)}) async-start(), calls=%async_computation.5 | async-start | bytes 5242880 | tf_op jit(solution)/shard_map/all_gather | solution.py:104
  361.3 5.4 copy-start.3
  361.3 5.4 copy-start.5
  467.6 59.9 %slice-start = ((s8[8388608]{0:T(1024)(128)(4,1)}), s8[4194304]{0:T(1024)(128)(4,1)S(1)}, s32[]{:S(2)}) async-start(s8[8388608]{0:T(1024)(128)(4,1)} %bitcast.109), calls=%async_computation.6 | async-start | bytes 8388608
  526.3 2.2 slice-start.1
  733.2 18.9 %copy-start.1 = (bf16[16,2,256,128]{3,2,1,0:T(8,128)(2,1)S(1)}, bf16[16,2,256,128]{3,2,1,0:T(8,128)(2,1)}, u32[]{:S(2)}) copy-start(bf16[16,2,256,128]{3,2,1,0:T(8,128)(2,1)} %param.8) | copy-start | bytes 6291460
Sparse Core Ops, SparseCore 0:
  107.9 48.5 all-gather.4
  383.0 44.5 all-gather.6
